TPU v7x, 256 devices: a whole 4x4x8 slice. The times are simulated.
256 devices in a mesh: frame: 32 (over x, z), row: 8 (over y, core).
Axes of the slice: x: 4, y: 4, z: 8, core: 2. Of those that a mesh axis runs over, the one named last changes fastest.
Arguments:
- frames_in: bfloat16 [32, 128, 64, 1152], P('frame', 'row'), may hold values from -6 to 6
- spatial_qkv: bfloat16 [1152, 1728], replicated
- spatial_out: bfloat16 [576, 1152], replicated, may hold values from -0.8984375 to 0.8984375
- temporal_qkv: bfloat16 [1152, 1728], replicated
- temporal_out: bfloat16 [576, 1152], replicated, may hold values from -0.8984375 to 0.8984375
- key_tiles: int32 [32, 128, 9], P('frame', 'row'), may hold values from 0 to 127, as said below
- tile_counts: int32 [32, 128], P('frame', 'row'), may hold values from 1 to 9, as said below
Outputs:
- frames_out: bfloat16 [32, 128, 64, 1152], P('frame', 'row')
Inputs may be any that keep to these rules, and one draw needn't show every extreme that they name: `key_tiles`: for query tile t, whose tile row is t // 4 and tile column t % 4, the first tile_counts entries name distinct tiles whose tile row and tile column each differ from t's by at most one; later entries equal t. `tile_counts`: at most the number of tiles within one tile row and one tile column of the query tile.
All inputs are finite; a program needn't handle non-finite values.
Results may differ from a plain program's by a relative error of at most 0.019.
Values may be sent and summed in bfloat16 or wider, within the bound.
A program may use at most 128 MiB of HBM per device.

v0:
```python
import jax
import jax.numpy as jnp
from jax import lax
from jax.sharding import PartitionSpec as P

HEADS = 8
HD = 72
TH = 4
TW = 16


NORM_EPS = 1e-06


def padded(x, sides, width):
    for axis, dim in sides:
        size, length = (lax.axis_size(axis), x.shape[dim])
        up = [(i, (i + 1) % size) for i in range(size - 1)]
        down = [(j, i) for i, j in up]
        last = lax.slice_in_dim(x, length - width, length, axis=dim)
        first = lax.slice_in_dim(x, 0, width, axis=dim)
        before = lax.ppermute(last, axis, up)
        after = lax.ppermute(first, axis, down)
        x = jnp.concatenate([before, x, after], axis=dim)
    return x


def layer_norm(values):
    values = values.astype(jnp.float32)
    centred = values - jnp.mean(values, axis=-1, keepdims=True)
    spread = jnp.mean(centred * centred, axis=-1, keepdims=True)
    return (centred * lax.rsqrt(spread + NORM_EPS)).astype(jnp.bfloat16)


def softmax_rows(scores):
    top = jnp.max(scores, axis=-1, keepdims=True)
    expo = jnp.exp(scores - top)
    return (expo / jnp.sum(expo, axis=-1, keepdims=True)).astype(jnp.bfloat16)


def temporal_core(item_set):
    frame_num, pos_num = (item_set.shape[0], item_set.shape[2])
    pieces = item_set.reshape(frame_num, pos_num, 3, HEADS, HD)
    scores = jnp.einsum(
        "fphd,gphd->phfg", pieces[:, :, 0], pieces[:, :, 1], preferred_element_type=jnp.float32
    ) * HD ** (-0.5)
    weights = softmax_rows(scores)
    result = jnp.einsum(
        "phfg,gphd->fphd", weights, pieces[:, :, 2], preferred_element_type=jnp.float32
    )
    return result.astype(jnp.bfloat16).reshape(frame_num, 1, pos_num, HEADS * HD)


def body(frames_in, spatial_qkv, spatial_out, temporal_qkv, temporal_out, key_tiles, tile_counts):
    inner_dim = HEADS * HD
    rows_dev = frames_in.shape[1]
    columns = frames_in.shape[2]
    feat_num = frames_in.shape[3]
    tile_rows = rows_dev // TH
    tile_cols = columns // TW
    slab = TH * columns
    pixels = rows_dev * columns
    frame_in = frames_in[0]
    normed = layer_norm(frame_in).reshape(pixels, feat_num)
    qkv_heads = spatial_qkv.reshape(feat_num, 3, HEADS, HD)
    projected = jnp.einsum(
        "te,echk->chkt", normed, qkv_heads, preferred_element_type=jnp.float32
    ).astype(jnp.bfloat16)
    queries = projected[0]
    keyval = projected[1:]
    extended = padded(keyval, (("row", 3),), slab)
    targets = key_tiles[0]
    counts = tile_counts[0]
    tile_num = targets.shape[0]
    slot_num = targets.shape[1]
    ext_row = targets // tile_cols - lax.axis_index("row") * tile_rows + 1
    own_row = jnp.arange(tile_num, dtype=jnp.int32) // tile_cols
    cand_id = (ext_row - own_row[:, None]) * tile_cols + targets % tile_cols
    live = jnp.arange(slot_num, dtype=jnp.int32)[None, :] < counts[:, None]
    cand_all = jnp.arange(3 * tile_cols, dtype=jnp.int32)
    allowed = jnp.any(live[:, :, None] & (cand_id[:, :, None] == cand_all[None, None, :]), axis=1)
    allowed = allowed.astype(jnp.float32).reshape(tile_rows, tile_cols, 3 * tile_cols)
    query_pos = jnp.arange(slab, dtype=jnp.int32)
    query_pick = (query_pos % columns // TW)[:, None] == jnp.arange(tile_cols, dtype=jnp.int32)[
        None, :
    ]
    query_pick = query_pick.astype(jnp.float32)
    key_pos = jnp.arange(3 * slab, dtype=jnp.int32)
    key_tile = key_pos // columns // TH * tile_cols + key_pos % columns // TW
    key_pick = (key_tile[None, :] == cand_all[:, None]).astype(jnp.float32)
    out_heads = spatial_out.reshape(HEADS, HD, feat_num)

    def tile_row_attend(row_num):
        query_blk = lax.dynamic_slice_in_dim(queries, row_num * slab, slab, 2)
        kv_blk = lax.dynamic_slice_in_dim(extended, row_num * slab, 3 * slab, 3)
        table = lax.dynamic_index_in_dim(allowed, row_num, 0, keepdims=False)
        visible = jnp.dot(jnp.dot(query_pick, table), key_pick) > 0.5
        scores = jnp.einsum(
            "hdq,hdk->hqk", query_blk, kv_blk[0], preferred_element_type=jnp.float32
        ) * HD ** (-0.5)
        scores = jnp.where(visible[None], scores, -1e30)
        weights = softmax_rows(scores)
        heads_out = jnp.einsum(
            "hqk,hdk->hdq", weights, kv_blk[1], preferred_element_type=jnp.float32
        ).astype(jnp.bfloat16)
        return jnp.einsum("hdq,hde->qe", heads_out, out_heads, preferred_element_type=jnp.float32)

    branch = lax.map(tile_row_attend, jnp.arange(tile_rows, dtype=jnp.int32))
    mixed_one = (frame_in.astype(jnp.float32) + branch.reshape(rows_dev, columns, feat_num)).astype(
        jnp.bfloat16
    )
    peer_count = lax.axis_size("frame")
    group_len = pixels // peer_count
    normed_two = layer_norm(mixed_one).reshape(1, peer_count, group_len, -1)
    proj_two = jnp.dot(
        normed_two.reshape(pixels, -1), temporal_qkv, preferred_element_type=jnp.float32
    )
    proj_two = proj_two.astype(jnp.bfloat16).reshape(1, peer_count, group_len, 3 * inner_dim)
    regrouped = temporal_core(
        lax.all_to_all(proj_two, "frame", split_axis=1, concat_axis=0, tiled=True)
    )
    returned = lax.all_to_all(regrouped, "frame", split_axis=0, concat_axis=1, tiled=True)
    branch_two = jnp.dot(
        returned.reshape(pixels, inner_dim), temporal_out, preferred_element_type=jnp.float32
    )
    result = (mixed_one.astype(jnp.float32) + branch_two.reshape(rows_dev, columns, -1)).astype(
        jnp.bfloat16
    )
    return result[None]


def solution(mesh):
    in_specs = (
        P("frame", "row", None, None),
        P(),
        P(),
        P(),
        P(),
        P("frame", "row", None),
        P("frame", "row"),
    )
    out_specs = P("frame", "row", None, None)
    return jax.shard_map(body, mesh=mesh, in_specs=in_specs, out_specs=out_specs, check_vma=False)
```

profile of v0, /device:TPU:8, one launch (start us, length us, event | category | flops | bytes accessed | tf_op | source)
XLA Modules:
  0.0 322.7 jit_solution(11434496910090724368)
XLA Ops:
  0.0 2.2 convert_reduce_fusion.1
  4.4 4.8 %fusion.89 = f32[1024,1728]{0,1:S(1)} fusion(bf16[1024,1152]{1,0:T(8,128)(2,1)S(1)} %bitcast.132, bf16[1152,1728]{0,1:T(8,128)(2,1)S(1)} %copy-done.7), kind=kOutput, calls=%fused_computation.142 | convolution fusion | flops 4076863488 | bytes 13418496
  10.9 1.9 collective-permute-start
  12.8 3.8 %collective-permute-start.1 = (bf16[2,8,72,256]{3,2,1,0:T(8,128)(2,1)}, bf16[2,8,72,256]{3,2,1,0:T(8,128)(2,1)}, u32[]{:S(2)}, u32[]{:S(2)}) collective-permute-start(bf16[2,8,72,256]{3,2,1,0:T(8,128)(2,1)} %get-tuple-element.102), channel_id=1, source_target_pairs={{1,0},{2,1},{3,2},{4,3},{5,4},{6,5},{7,6},{9,8},{10,9},{11,10},{12... | collective-permute-start | bytes 1769480 | tf_op jit(solution)/shard_map/ppermute | solution.py:23
  18.4 3.9 %collective-permute-done = bf16[2,8,72,256]{3,2,1,0:T(8,128)(2,1)S(1)} collective-permute-done((bf16[2,8,72,256]{3,2,1,0:T(8,128)(2,1)}, bf16[2,8,72,256]{3,2,1,0:T(8,128)(2,1)S(1)}, u32[]{:S(2)}, u32[]{:S(2)}) %collective-permute-start) | collective-permute-done | bytes 589856 | tf_op jit(solution)/shard_map/ppermute | solution.py:22
  22.3 1.9 collective-permute-done.1
  24.1 2.8 pad_maximum_fusion
  27.0 99.5 %while.11 = (s32[]{:T(128)}, f32[4,256,1152]{2,1,0:T(8,128)}, s32[4]{0:T(128)S(1)}, bf16[2,8,72,1536]{3,2,1,0:T(8,128)(2,1)}, bf16[4,4,12]{2,1,0:T(4,128)(2,1)S(...) while((s32[]{:T(128)}, f32[4,256,1152]{2,1,0:T(8,128)}, ...), condition=%wide.region_6.7_spmd.clone, body=%wide.region_3.6_spmd.clone.sunk | while | flops 810414848 | bytes 30153512 | solution.py:108
  28.2 4.8 %fusion.110 = f32[8,256,768]{2,1,0:T(8,128)} fusion(bf16[2,8,72,1536]{3,2,1,0:T(8,128)(2,1)} %get-tuple-element.201, s32[]{:T(128)S(6)} %select_n.184, bf16[8,72,1024]{2,1,0:T(8,128)(2,1)S(1)} %get-tuple-element.203, s32[]{:T(128)S(6)} %select_n.185), kind=kOutput, calls=%fused_computation.17.clone.1 | convolution fusion | flops 226492416 | bytes 7471112 | tf_op jit(solution)/shard_map/while/body/eval_jaxpr/hdq,hdk->hqk/dot_general | solution.py:98
  35.6 10.2 %fusion.111 = (f32[8,256]{1,0:T(8,128)S(1)}, f32[8,256,768]{2,1,0:T(8,128)}) fusion(f32[8,256,768]{2,1,0:T(8,128)} %fusion.110, pred[256,768]{1,0:T(8,128)(4,1)S(1)} %convolution_compare_fusion.2), kind=kOutput, calls=%fused_computation.138.clone.1 | output fusion | flops 9437951 | bytes 12787712 | tf_op jit(solution)/shard_map/while/body/eval_jaxpr/sub | solution.py:37
  45.7 6.2 %fusion.112 = f32[4,256,1152]{2,1,0:T(8,128)} fusion(f32[4,256,1152]{2,1,0:T(8,128)} %get-tuple-element.183, s32[]{:T(128)} %get-tuple-element.182, bf16[8,72,1152]{2,1,0:T(8,128)(2,1)} %get-tuple-element.204, f32[8,256,768]{2,1,0:T(8,128)} %get-tuple-element.164, f32[8,256]{1,0:T(8,128)S(1)} %get-tuple-element.165, ...), kind=kOutput, calls=%fused_computation.12.clone.1 | convolution fusion | flops 569524224 | bytes 9691656 | tf_op jit(solution)/shard_map/while/body/eval_jaxpr/hdq,hde->qe/dot_general | solution.py:106
  53.1 4.9 %fusion.110 = f32[8,256,768]{2,1,0:T(8,128)} fusion(bf16[2,8,72,1536]{3,2,1,0:T(8,128)(2,1)} %get-tuple-element.201, s32[]{:T(128)S(6)} %select_n.184, bf16[8,72,1024]{2,1,0:T(8,128)(2,1)S(1)} %get-tuple-element.203, s32[]{:T(128)S(6)} %select_n.185), kind=kOutput, calls=%fused_computation.17.clone.1 | convolution fusion | flops 226492416 | bytes 7471112 | tf_op jit(solution)/shard_map/while/body/eval_jaxpr/hdq,hdk->hqk/dot_general | solution.py:98
  60.5 10.2 %fusion.111 = (f32[8,256]{1,0:T(8,128)S(1)}, f32[8,256,768]{2,1,0:T(8,128)}) fusion(f32[8,256,768]{2,1,0:T(8,128)} %fusion.110, pred[256,768]{1,0:T(8,128)(4,1)S(1)} %convolution_compare_fusion.2), kind=kOutput, calls=%fused_computation.138.clone.1 | output fusion | flops 9437951 | bytes 12787712 | tf_op jit(solution)/shard_map/while/body/eval_jaxpr/sub | solution.py:37
  70.6 6.1 %fusion.112 = f32[4,256,1152]{2,1,0:T(8,128)} fusion(f32[4,256,1152]{2,1,0:T(8,128)} %get-tuple-element.183, s32[]{:T(128)} %get-tuple-element.182, bf16[8,72,1152]{2,1,0:T(8,128)(2,1)} %get-tuple-element.204, f32[8,256,768]{2,1,0:T(8,128)} %get-tuple-element.164, f32[8,256]{1,0:T(8,128)S(1)} %get-tuple-element.165, ...), kind=kOutput, calls=%fused_computation.12.clone.1 | convolution fusion | flops 569524224 | bytes 9691656 | tf_op jit(solution)/shard_map/while/body/eval_jaxpr/hdq,hde->qe/dot_general | solution.py:106
  78.0 4.9 %fusion.110 = f32[8,256,768]{2,1,0:T(8,128)} fusion(bf16[2,8,72,1536]{3,2,1,0:T(8,128)(2,1)} %get-tuple-element.201, s32[]{:T(128)S(6)} %select_n.184, bf16[8,72,1024]{2,1,0:T(8,128)(2,1)S(1)} %get-tuple-element.203, s32[]{:T(128)S(6)} %select_n.185), kind=kOutput, calls=%fused_computation.17.clone.1 | convolution fusion | flops 226492416 | bytes 7471112 | tf_op jit(solution)/shard_map/while/body/eval_jaxpr/hdq,hdk->hqk/dot_general | solution.py:98
  85.3 10.2 %fusion.111 = (f32[8,256]{1,0:T(8,128)S(1)}, f32[8,256,768]{2,1,0:T(8,128)}) fusion(f32[8,256,768]{2,1,0:T(8,128)} %fusion.110, pred[256,768]{1,0:T(8,128)(4,1)S(1)} %convolution_compare_fusion.2), kind=kOutput, calls=%fused_computation.138.clone.1 | output fusion | flops 9437951 | bytes 12787712 | tf_op jit(solution)/shard_map/while/body/eval_jaxpr/sub | solution.py:37
  95.5 6.1 %fusion.112 = f32[4,256,1152]{2,1,0:T(8,128)} fusion(f32[4,256,1152]{2,1,0:T(8,128)} %get-tuple-element.183, s32[]{:T(128)} %get-tuple-element.182, bf16[8,72,1152]{2,1,0:T(8,128)(2,1)} %get-tuple-element.204, f32[8,256,768]{2,1,0:T(8,128)} %get-tuple-element.164, f32[8,256]{1,0:T(8,128)S(1)} %get-tuple-element.165, ...), kind=kOutput, calls=%fused_computation.12.clone.1 | convolution fusion | flops 569524224 | bytes 9691656 | tf_op jit(solution)/shard_map/while/body/eval_jaxpr/hdq,hde->qe/dot_general | solution.py:106
  102.8 4.9 %fusion.110 = f32[8,256,768]{2,1,0:T(8,128)} fusion(bf16[2,8,72,1536]{3,2,1,0:T(8,128)(2,1)} %get-tuple-element.201, s32[]{:T(128)S(6)} %select_n.184, bf16[8,72,1024]{2,1,0:T(8,128)(2,1)S(1)} %get-tuple-element.203, s32[]{:T(128)S(6)} %select_n.185), kind=kOutput, calls=%fused_computation.17.clone.1 | convolution fusion | flops 226492416 | bytes 7471112 | tf_op jit(solution)/shard_map/while/body/eval_jaxpr/hdq,hdk->hqk/dot_general | solution.py:98
  110.2 10.2 %fusion.111 = (f32[8,256]{1,0:T(8,128)S(1)}, f32[8,256,768]{2,1,0:T(8,128)}) fusion(f32[8,256,768]{2,1,0:T(8,128)} %fusion.110, pred[256,768]{1,0:T(8,128)(4,1)S(1)} %convolution_compare_fusion.2), kind=kOutput, calls=%fused_computation.138.clone.1 | output fusion | flops 9437951 | bytes 12787712 | tf_op jit(solution)/shard_map/while/body/eval_jaxpr/sub | solution.py:37
  120.3 6.1 %fusion.112 = f32[4,256,1152]{2,1,0:T(8,128)} fusion(f32[4,256,1152]{2,1,0:T(8,128)} %get-tuple-element.183, s32[]{:T(128)} %get-tuple-element.182, bf16[8,72,1152]{2,1,0:T(8,128)(2,1)} %get-tuple-element.204, f32[8,256,768]{2,1,0:T(8,128)} %get-tuple-element.164, f32[8,256]{1,0:T(8,128)S(1)} %get-tuple-element.165, ...), kind=kOutput, calls=%fused_computation.12.clone.1 | convolution fusion | flops 569524224 | bytes 9691656 | tf_op jit(solution)/shard_map/while/body/eval_jaxpr/hdq,hde->qe/dot_general | solution.py:106
  126.4 3.7 %fusion.36 = bf16[1024,1152]{1,0:T(8,128)(2,1)S(1)} fusion(f32[4,256,1152]{2,1,0:T(8,128)} %get-tuple-element.52, bf16[1,16,64,1152]{3,2,1,0:T(8,128)(2,1)} %param.9), kind=kLoop, calls=%fused_computation.39 | loop fusion | flops 3538944 | bytes 9437184 | tf_op jit(solution)/shard_map/convert_element_type | solution.py:109
  133.7 7.1 %convolution_convert_fusion = bf16[1024,1728]{0,1:T(8,128)(2,1)} fusion(bf16[1152,1728]{0,1:T(8,128)(2,1)S(1)} %copy-done.8, bf16[1024,1152]{1,0:T(8,128)(2,1)S(1)} %fusion.36, f32[1024]{0:T(1024)S(1)} %bitcast.135, f32[1024]{0:T(1024)S(1)} %bitcast.136), kind=kOutput, calls=%fused_computation.54 | convolution fusion | flops 4083351552 | bytes 9887744 | tf_op jit(solution)/shard_map/dot_general | solution.py:115
  140.8 5.9 %copy.26 = bf16[1024,1728]{1,0:T(8,128)(2,1)} copy(bf16[1024,1728]{0,1:T(8,128)(2,1)} %convolution_convert_fusion) | data formatting | bytes 7077888 | tf_op jit(solution)/shard_map/convert_element_type | solution.py:118
  146.6 94.7 %all_to_all.8 = bf16[1,32,32,1728]{3,2,0,1:T(8,128)(2,1)} all-to-all(bf16[1,32,32,1728]{3,2,0,1:T(8,128)(2,1)} %bitcast.129), channel_id=1, replica_groups=mesh['frame'=32,'row'=8] {'frame'}, dimensions={1} | all-to-all | bytes 7077888 | tf_op jit(solution)/shard_map/all_to_all | solution.py:120
  241.4 11.2 %reshape.301 = bf16[32,32,3,8,72]{4,3,2,1,0:T(8,128)(2,1)} reshape(bf16[1,32,32,1728]{3,2,0,1:T(8,128)(2,1)} %all_to_all.8) | data formatting | bytes 7077888 | tf_op jit(solution)/shard_map/reshape | solution.py:43
  252.5 3.6 %fusion.86 = (bf16[32,32,1,8,72]{4,3,2,1,0:T(8,128)(2,1)S(1)}, bf16[32,32,1,8,72]{4,3,2,1,0:T(8,128)(2,1)S(1)}, bf16[32,32,1,8,72]{4,3,2,1,0:T(8,128)(2,1)S(1)}) fusion(bf16[32,32,3,8,72]{4,3,2,1,0:T(8,128)(2,1)} %reshape.301), kind=kLoop, calls=%fused_computation.139 | loop fusion | bytes 7077888 | tf_op jit(solution)/shard_map/slice | solution.py:49
  256.2 2.7 fusion.49
  258.9 9.5 %fusion.88 = (f32[32,8,32]{2,1,0:T(8,128)S(1)}, f32[32,8,32,32]{2,3,1,0:T(8,128)S(1)}) fusion(f32[32,8,32,32]{2,3,1,0:T(8,128)S(1)} %fusion.49), kind=kOutput, calls=%fused_computation.141 | output fusion | flops 1048607 | bytes 2129920 | tf_op jit(solution)/shard_map/sub | solution.py:37
  268.4 1.9 convert_bitcast_fusion.1
  271.2 2.5 reshape.302
  273.7 42.4 %all_to_all.9 = bf16[32,1,32,576]{3,2,1,0:T(8,128)(2,1)S(1)} all-to-all(bf16[32,1,32,576]{3,2,1,0:T(8,128)(2,1)} %bitcast.131), channel_id=1, replica_groups=mesh['frame'=32,'row'=8] {'frame'}, dimensions={0} | all-to-all | bytes 2359296 | tf_op jit(solution)/shard_map/all_to_all | solution.py:122
  316.1 6.6 %fusion.43 = bf16[1,16,64,1152]{3,2,1,0:T(8,128)(2,1)} fusion(bf16[16,64,576]{2,1,0:T(8,128)(2,1)S(1)} %bitcast.133, f32[16,64,1152]{2,1,0:T(8,128)} %bitcast.128, bf16[1,16,64,1152]{3,2,1,0:T(8,128)(2,1)} %param.9, bf16[576,1152]{1,0:T(8,128)(2,1)S(1)} %copy-done), kind=kOutput, calls=%fused_computation.59 | convolution fusion | flops 1366032384 | bytes 11943936 | tf_op jit(solution)/shard_map/dot_general | solution.py:123
  (51 shorter events, 14.4 us)
Async XLA Ops:
  0.0 316.1 %copy-start = (bf16[576,1152]{1,0:T(8,128)(2,1)S(1)}, bf16[576,1152]{1,0:T(8,128)(2,1)}, u32[]{:S(2)}) copy-start(bf16[576,1152]{1,0:T(8,128)(2,1)} %param.13) | copy-start | bytes 3981316
  0.0 2.5 copy-start.1
  2.2 2.2 copy-start.7
  9.7 6.9 %copy-start.3 = (bf16[3,8,72,1024]{3,2,1,0:T(8,128)(2,1)}, bf16[3,8,72,1024]{3,2,1,0:T(8,128)(2,1)S(1)}, u32[]{:S(2)}) copy-start(bf16[3,8,72,1024]{3,2,1,0:T(8,128)(2,1)S(1)} %convert_bitcast_fusion) | copy-start | bytes 10616836
  9.8 6.9 %copy-start.6 = (s32[1,16]{1,0:T(1,128)S(1)}, s32[1,16]{1,0:T(1,128)}, u32[]{:S(2)}) copy-start(s32[1,16]{1,0:T(1,128)} %param.15) | copy-start | bytes 196
  9.8 6.9 %copy-start.5 = (s32[1,16,9]{1,0,2:T(1,128)S(1)}, s32[1,16,9]{1,0,2:T(1,128)}, u32[]{:S(2)}) copy-start(s32[1,16,9]{1,0,2:T(1,128)} %param.14) | copy-start | bytes 1732
  10.9 11.4 %collective-permute-start = (bf16[2,8,72,256]{3,2,1,0:T(8,128)(2,1)}, bf16[2,8,72,256]{3,2,1,0:T(8,128)(2,1)S(1)}, u32[]{:S(2)}, u32[]{:S(2)}) collective-permute-start(bf16[2,8,72,256]{3,2,1,0:T(8,128)(2,1)} %get-tuple-element.101), channel_id=1, source_target_pairs={{0,1},{1,2},{2,3},{3,4},{4,5},{5,6},{6,7},{8,9},{9,10},{10,11},{11... | collective-permute-start | bytes 1769480 | tf_op jit(solution)/shard_map/ppermute | solution.py:22
  12.8 11.3 %collective-permute-start.1 = (bf16[2,8,72,256]{3,2,1,0:T(8,128)(2,1)}, bf16[2,8,72,256]{3,2,1,0:T(8,128)(2,1)}, u32[]{:S(2)}, u32[]{:S(2)}) collective-permute-start(bf16[2,8,72,256]{3,2,1,0:T(8,128)(2,1)} %get-tuple-element.102), channel_id=1, source_target_pairs={{1,0},{2,1},{3,2},{4,3},{5,4},{6,5},{7,6},{9,8},{10,9},{11,10},{12... | collective-permute-start | bytes 1769480 | tf_op jit(solution)/shard_map/ppermute | solution.py:23
  16.8 7.3 %slice-start = ((bf16[3,8,72,1024]{3,2,1,0:T(8,128)(2,1)}), bf16[2,8,72,1024]{3,2,1,0:T(8,128)(2,1)S(1)}, s32[]{:S(2)}) async-start(bf16[3,8,72,1024]{3,2,1,0:T(8,128)(2,1)} %copy-done.3), calls=%async_computation.2 | async-start | bytes 4718592 | tf_op jit(solution)/shard_map/slice | solution.py:70
  126.4 3.8 %copy-start.2 = (bf16[1,16,64,1152]{3,2,1,0:T(8,128)(2,1)S(1)}, bf16[1,16,64,1152]{3,2,1,0:T(8,128)(2,1)}, u32[]{:S(2)}) copy-start(bf16[1,16,64,1152]{3,2,1,0:T(8,128)(2,1)} %param.9) | copy-start | bytes 7077892
  126.4 5.1 %copy-start.4 = (f32[4,256,1152]{2,1,0:T(8,128)S(1)}, f32[4,256,1152]{2,1,0:T(8,128)}, u32[]{:S(2)}) copy-start(f32[4,256,1152]{2,1,0:T(8,128)} %get-tuple-element.52) | copy-start | bytes 14155780
  131.6 2.1 copy-start.8
where the time goes:
time: 324 us; the launch traced here: 323 us
  blocking collectives  137 us (42%)
  matrix products  69.2 us (21%)
  other arithmetic  62.3 us (19%)
  local copies, waits for them, and re-layouts  31.9 us (10%)
  loops' own time  10.4 us (3%)
  starting transfers between devices  5.73 us (2%)
  waiting for transfers between devices  5.73 us (2%)
    all_to_all x1, blocking collectives, body(): lax.all_to_all(proj_two, 'frame', split_axis=1, concat_axis=0, tiled=True)  94.7 us
    sub x5, other arithmetic, softmax_rows(): expo = jnp.exp(scores - top)  50.1 us
    all_to_all x1, blocking collectives, body(): lax.all_to_all(regrouped, 'frame', split_axis=0, concat_axis=1, tiled=True)  42.4 us
    dot_general x4, matrix products, tile_row_attend(): jnp.einsum('hdq,hde->qe', heads_out, out_heads, preferred_element_type=jn...  24.4 us
    dot_general x4, matrix products, tile_row_attend(): jnp.einsum('hdq,hdk->hqk', query_blk, kv_blk[0], preferred_element_type=j...  19.4 us
    reshape x1, local copies, waits for them, and re-layouts, temporal_core(): pieces = item_set.reshape(frame_num, pos_num, 3, HEADS, HD)  11.2 us
    another operation x1, loops' own time, body(): branch = lax.map(tile_row_attend, jnp.arange(tile_rows, dtype=jnp.int32))  10.4 us
    dot_general x1, matrix products, body(): jnp.dot(normed_two.reshape(pixels, -1), temporal_qkv, preferred_element_t...  7.08 us
  transfers between devices with their start and end apart: 2, of which 2 were waited for; matrix products, arithmetic and copies ran while one was open for 1% of the time, Pallas kernels for 0%

commit v1 on v0

v1 whole, which is shorter than its diff:
```python
import functools
import math

import jax
import jax.numpy as jnp
from jax import lax
from jax.experimental import pallas as pl
from jax.experimental.pallas import tpu as pltpu
from jax.sharding import PartitionSpec as P

HEADS = 8
HD = 72
TH = 4
TW = 16
INNER = HEADS * HD
PADDED = 640
EPS = 1e-06
NEG = -1e30
SCALE = HD ** (-0.5) * math.log2(math.e)
MESH = pl.DeviceIdType.MESH
F32 = jnp.float32
BF16 = jnp.bfloat16
NT = (((1,), (1,)), ((), ()))


def window(head):
    first, last = head * HD, (head + 1) * HD
    low = first // 128 * 128
    high = -(-last // 128) * 128
    return low, high, first - low, last - low


def layer_norm(values):
    centred = values - jnp.mean(values, axis=-1, keepdims=True)
    spread = jnp.mean(centred * centred, axis=-1, keepdims=True)
    return (centred * lax.rsqrt(spread + EPS)).astype(BF16)


def attend(load_q, load_k, load_v, keep, fill):
    columns = [None] * (PADDED // 128)
    for head in range(HEADS):
        low, high, first, last = window(head)
        query = load_q(low, high)
        lane = lax.broadcasted_iota(jnp.int32, query.shape, 1)
        query = jnp.where((lane >= first) & (lane < last), query, jnp.zeros_like(query))
        scores = lax.dot_general(query, load_k(low, high), NT, preferred_element_type=F32)
        scores = jnp.where(keep, scores, fill)
        top = jnp.max(scores, axis=-1, keepdims=True)
        expo = jnp.exp2(scores - top)
        total = jnp.sum(expo, axis=-1, keepdims=True)
        result = jnp.dot(expo.astype(BF16), load_v(low, high), preferred_element_type=F32)
        result = result * (1.0 / total)
        for part in range((high - low) // 128):
            piece = result[:, part * 128 : (part + 1) * 128]
            at = low // 128 + part
            if columns[at] is None:
                columns[at] = piece
            else:
                spot = lax.broadcasted_iota(jnp.int32, piece.shape, 1) + part * 128
                columns[at] = jnp.where(spot >= first, piece, columns[at])
    spot = lax.broadcasted_iota(jnp.int32, columns[-1].shape, 1)
    columns[-1] = jnp.where(spot < INNER - PADDED + 128, columns[-1], 0.0)
    return jnp.concatenate(columns, axis=1)


def pad_qkv(raw, out):
    depth = raw.shape[0]
    zeros = jnp.zeros((128, PADDED - INNER), BF16)

    def step(i, carry):
        rows = pl.ds(pl.multiple_of(i * 128, 128), 128)
        for part in range(3):
            piece = raw[rows, part * INNER : (part + 1) * INNER]
            out[rows, part * PADDED : (part + 1) * PADDED] = jnp.concatenate([piece, zeros], axis=1)
        return carry

    lax.fori_loop(0, depth // 128, step, 0)


def kernel(
    frames, rows_axis,
    key_tiles, tile_counts, x_hbm, sqkv_hbm, sout_hbm, tqkv_hbm, tout_hbm, out_hbm,
    xbuf, halo, raw_s, raw_t, w_s, w_t, o_s, o_t, qbuf, kbuf, vbuf,
    mixed, landed, heads, back, obuf,
    load_sem, halo_send, halo_recv, go_send, go_recv, back_send, back_recv, store_sem,
):
    frame = lax.axis_index("frame")
    row = lax.axis_index("row")
    above = lax.rem(row + rows_axis - 1, rows_axis)
    below = lax.rem(row + 1, rows_axis)
    feat = x_hbm.shape[-1]
    columns = x_hbm.shape[1]
    slab = TH * columns
    tile_rows = x_hbm.shape[0] // TH
    tile_cols = columns // TW
    tile_len = TH * TW
    group = slab // frames

    barrier = pltpu.get_barrier_semaphore()

    def greet(i, carry):
        pl.semaphore_signal(
            barrier, inc=1, device_id=(lax.rem(frame + i, frames), row), device_id_type=MESH
        )
        return carry

    lax.fori_loop(1, frames, greet, 0)
    for peer in (above, below):
        pl.semaphore_signal(barrier, inc=1, device_id=(frame, peer), device_id_type=MESH)

    loads = [
        pltpu.make_async_copy(src, dst, load_sem.at[i])
        for i, (src, dst) in enumerate(
            (
                (sqkv_hbm, raw_s),
                (x_hbm, xbuf),
                (sout_hbm, o_s.at[pl.ds(0, INNER)]),
                (tqkv_hbm, raw_t),
                (tout_hbm, o_t.at[pl.ds(0, INNER)]),
            )
        )
    ]
    for load in loads:
        load.start()
    pad_rows = jnp.zeros((PADDED - INNER, feat), BF16)
    o_s[INNER:, :] = pad_rows
    o_t[INNER:, :] = pad_rows

    pl.semaphore_wait(barrier, frames + 1)
    send_down = pltpu.make_async_remote_copy(
        x_hbm.at[pl.ds((tile_rows - 1) * TH, TH)], halo.at[0], halo_send.at[0], halo_recv.at[0],
        device_id=(frame, below), device_id_type=MESH,
    )
    send_up = pltpu.make_async_remote_copy(
        x_hbm.at[pl.ds(0, TH)], halo.at[1], halo_send.at[1], halo_recv.at[1],
        device_id=(frame, above), device_id_type=MESH,
    )
    send_down.start()
    send_up.start()

    loads[0].wait()
    pad_qkv(raw_s, w_s)
    loads[1].wait()

    def tiled(ref, first):
        return jnp.concatenate(
            [
                ref[pl.ds(first, TH), c * TW : (c + 1) * TW, :].reshape(tile_len, feat)
                for c in range(tile_cols)
            ],
            axis=0,
        )

    def project(i, carry):
        normed = layer_norm(tiled(xbuf, i * TH).astype(F32))
        result = jnp.dot(normed, w_s[...], preferred_element_type=F32)
        qbuf[i] = (result[:, :PADDED] * SCALE).astype(BF16)
        kbuf[i + 1] = result[:, PADDED : 2 * PADDED].astype(BF16)
        vbuf[i + 1] = result[:, 2 * PADDED :].astype(BF16)
        return carry

    def spatial(i):
        halves = []
        for half in range(2):
            marks = []
            for c in (2 * half, 2 * half + 1):
                tile = i * tile_cols + c
                count = tile_counts[0, tile]
                spot = lax.broadcasted_iota(jnp.int32, (tile_len, 9 * tile_len), 1) // tile_len
                mark = jnp.zeros((tile_len, 9 * tile_len), jnp.int32)
                for slot in range(key_tiles.shape[2]):
                    target = key_tiles[0, tile, slot]
                    down = (target // tile_cols) - (row * tile_rows + i) + 1
                    name = down * 3 + target % tile_cols - half
                    name = jnp.where(slot < count, name, -1)
                    mark = jnp.where(spot == name, 1, mark)
                marks.append(mark)
            keep = jnp.concatenate(marks, axis=0) > 0
            at = half * tile_len

            def load_q(low, high):
                return qbuf[i, 2 * at : 2 * at + 2 * tile_len, low:high]

            def load_keys(ref):
                def load(low, high):
                    return jnp.concatenate(
                        [ref[i + d, at : at + 3 * tile_len, low:high] for d in range(3)], axis=0
                    )

                return load

            halves.append(attend(load_q, load_keys(kbuf), load_keys(vbuf), keep, NEG).astype(BF16))
        attended = jnp.concatenate(halves, axis=0)
        branch = jnp.dot(attended, o_s[...], preferred_element_type=F32)
        result = tiled(xbuf, i * TH).astype(F32) + branch
        mixed[i] = result.reshape(frames, group, feat).astype(BF16)
        landed[i, frame] = mixed[i, frame]

        def send(k, carry):
            peer = lax.rem(frame + k, frames)
            pltpu.make_async_remote_copy(
                mixed.at[i, peer], landed.at[i, frame], go_send.at[i], go_recv.at[i],
                device_id=(peer, row), device_id_type=MESH,
            ).start()
            return carry

        lax.fori_loop(1, frames, send, 0)

    def temporal(i):
        pltpu.make_async_copy(
            landed.at[i, pl.ds(0, frames - 1)], landed.at[i, pl.ds(0, frames - 1)], go_recv.at[i]
        ).wait()
        normed = layer_norm(landed[i].astype(F32).reshape(slab, feat))
        result = jnp.dot(normed, w_t[...], preferred_element_type=F32)
        queries = (result[:, :PADDED] * SCALE).astype(BF16)
        key_vecs = result[:, PADDED : 2 * PADDED].astype(BF16)
        val_vecs = result[:, 2 * PADDED :].astype(BF16)
        mine = lax.broadcasted_iota(jnp.int32, (slab, slab), 0) % group
        theirs = lax.broadcasted_iota(jnp.int32, (slab, slab), 1) % group
        attended = attend(
            lambda low, high: queries[:, low:high],
            lambda low, high: key_vecs[:, low:high],
            lambda low, high: val_vecs[:, low:high],
            mine == theirs,
            -jnp.inf,
        )
        heads[i] = attended.reshape(frames, group, PADDED).astype(BF16)
        back[i, frame] = heads[i, frame]

        def send(k, carry):
            peer = lax.rem(frame + k, frames)
            pltpu.make_async_remote_copy(
                heads.at[i, peer], back.at[i, frame], back_send.at[i], back_recv.at[i],
                device_id=(peer, row), device_id_type=MESH,
            ).start()
            return carry

        lax.fori_loop(1, frames, send, 0)

    def finish(i):
        pltpu.make_async_copy(
            back.at[i, pl.ds(0, frames - 1)], back.at[i, pl.ds(0, frames - 1)], back_recv.at[i]
        ).wait()
        attended = back[i].astype(F32).reshape(slab, PADDED).astype(BF16)
        branch = jnp.dot(attended, o_t[...], preferred_element_type=F32)
        result = (mixed[i].astype(F32).reshape(slab, feat) + branch).astype(BF16)
        for c in range(tile_cols):
            obuf[pl.ds(i * TH, TH), c * TW : (c + 1) * TW, :] = result[
                c * tile_len : (c + 1) * tile_len
            ].reshape(TH, TW, feat)
        pltpu.make_async_copy(
            obuf.at[pl.ds(i * TH, TH)], out_hbm.at[pl.ds(i * TH, TH)], store_sem.at[i]
        ).start()

    lax.fori_loop(0, tile_rows, project, 0)
    loads[2].wait()

    def inner_rows(n, carry):
        spatial(n)
        return carry

    lax.fori_loop(1, tile_rows - 1, inner_rows, 0)

    send_down.wait()
    send_up.wait()

    def project_halo(n, carry):
        normed = layer_norm(tiled(halo.at[n], 0).astype(F32))
        result = jnp.dot(normed, w_s[:, PADDED:], preferred_element_type=F32)
        place = n * (tile_rows + 1)
        kbuf[place] = result[:, :PADDED].astype(BF16)
        vbuf[place] = result[:, PADDED:].astype(BF16)
        return carry

    lax.fori_loop(0, 2, project_halo, 0)

    def outer_rows(n, carry):
        spatial(n * (tile_rows - 1))
        return carry

    lax.fori_loop(0, 2, outer_rows, 0)

    loads[3].wait()
    pad_qkv(raw_t, w_t)
    loads[4].wait()

    def order(n):
        return lax.rem(n + 1, tile_rows)

    def temporal_rows(n, carry):
        temporal(order(n))
        return carry

    lax.fori_loop(0, tile_rows, temporal_rows, 0)

    def finish_rows(n, carry):
        finish(order(n))
        return carry

    lax.fori_loop(0, tile_rows, finish_rows, 0)

    for i in range(tile_rows):
        block = landed.at[i, pl.ds(0, frames - 1)]
        pltpu.make_async_copy(block, block, go_send.at[i]).wait()
        block = back.at[i, pl.ds(0, frames - 1)]
        pltpu.make_async_copy(block, block, back_send.at[i]).wait()
        pltpu.make_async_copy(
            obuf.at[pl.ds(i * TH, TH)], out_hbm.at[pl.ds(i * TH, TH)], store_sem.at[i]
        ).wait()


def body(frames_in, spatial_qkv, spatial_out, temporal_qkv, temporal_out, key_tiles, tile_counts):
    frames = lax.axis_size("frame")
    rows_axis = lax.axis_size("row")
    rows, columns, feat = frames_in.shape[1:]
    slab = TH * columns
    tile_rows = rows // TH
    group = slab // frames
    dma = pltpu.SemaphoreType.DMA
    smem = pl.BlockSpec(memory_space=pltpu.SMEM)
    hbm = pl.BlockSpec(memory_space=pl.ANY)
    result = pl.pallas_call(
        functools.partial(kernel, frames, rows_axis),
        out_shape=jax.ShapeDtypeStruct((rows, columns, feat), BF16),
        in_specs=[smem, smem, hbm, hbm, hbm, hbm, hbm],
        out_specs=hbm,
        scratch_shapes=[
            pltpu.VMEM((rows, columns, feat), BF16),
            pltpu.VMEM((2, TH, columns, feat), BF16),
            pltpu.VMEM((feat, 3 * INNER), BF16),
            pltpu.VMEM((feat, 3 * INNER), BF16),
            pltpu.VMEM((feat, 3 * PADDED), BF16),
            pltpu.VMEM((feat, 3 * PADDED), BF16),
            pltpu.VMEM((PADDED, feat), BF16),
            pltpu.VMEM((PADDED, feat), BF16),
            pltpu.VMEM((tile_rows, slab, PADDED), BF16),
            pltpu.VMEM((tile_rows + 2, slab, PADDED), BF16),
            pltpu.VMEM((tile_rows + 2, slab, PADDED), BF16),
            pltpu.VMEM((tile_rows, frames, group, feat), BF16),
            pltpu.VMEM((tile_rows, frames, group, feat), BF16),
            pltpu.VMEM((tile_rows, frames, group, PADDED), BF16),
            pltpu.VMEM((tile_rows, frames, group, PADDED), BF16),
            pltpu.VMEM((rows, columns, feat), BF16),
            dma((5,)),
            dma((2,)),
            dma((2,)),
            dma((tile_rows,)),
            dma((tile_rows,)),
            dma((tile_rows,)),
            dma((tile_rows,)),
            dma((tile_rows,)),
        ],
        compiler_params=pltpu.CompilerParams(
            collective_id=0, has_side_effects=True, vmem_limit_bytes=67043328
        ),
    )(
        key_tiles, tile_counts, frames_in[0],
        spatial_qkv, spatial_out, temporal_qkv, temporal_out,
    )
    return result[None]


def solution(mesh):
    in_specs = (
        P("frame", "row", None, None),
        P(),
        P(),
        P(),
        P(),
        P("frame", "row", None),
        P("frame", "row"),
    )
    out_specs = P("frame", "row", None, None)
    return jax.shard_map(body, mesh=mesh, in_specs=in_specs, out_specs=out_specs, check_vma=False)
```

time: 324 us -> 123 us (0.38)
  blocking collectives: 137 us -> 0 us
  Pallas kernels: 0 us -> 105 us
  matrix products: 69.2 us -> 0 us
  other arithmetic: 62.3 us -> 0 us
  local copies, waits for them, and re-layouts: 31.9 us -> 17.5 us
  loops' own time: 10.4 us -> 0 us
  starting transfers between devices: 5.73 us -> 0 us
  waiting for transfers between devices: 5.73 us -> 0 us
    all_to_all x2 -> x0, blocking collectives: 137 us -> none  [the longest x1 94.7 us: body(): lax.all_to_all(proj_two, 'frame', split_axis=1, concat_axis=0, tiled=True)]
    pallas_call x0 -> x1, Pallas kernels: none -> 105 us  [body(): pl.pallas_call(functools.partial(kernel, frames, rows_axis), out_shape=ja...]
    dot_general x16 -> x0, matrix products: 64.4 us -> none  [the longest x4 24.4 us: tile_row_attend(): jnp.einsum('hdq,hde->qe', heads_out, out_heads, preferred_element_type=jn...]
    sub x5 -> x0, other arithmetic: 50.1 us -> none  [softmax_rows(): expo = jnp.exp(scores - top)]
    unnamed x20 -> x4, local copies, waits for them, and re-layouts: 2.95 us -> 17.5 us
    reshape x2 -> x0, local copies, waits for them, and re-layouts: 13.7 us -> none  [the longest x1 11.2 us: temporal_core(): pieces = item_set.reshape(frame_num, pos_num, 3, HEADS, HD)]
    another operation x1 -> x0, loops' own time: 10.4 us -> none  [body(): branch = lax.map(tile_row_attend, jnp.arange(tile_rows, dtype=jnp.int32))]
    convert_element_type x2 -> x0, local copies, waits for them, and re-layouts: 6.67 us -> none  [the longest x1 5.85 us: body(): proj_two.astype(jnp.bfloat16)]
  transfers between devices with their start and end apart: 2 -> 0, of which waited for: 2 -> 0; matrix products, arithmetic and copies ran while one was open for 1% -> 0% of each run, Pallas kernels for 0% -> 0%
where the time goes in v1:
time: 123 us
  Pallas kernels  105 us (85%)
  local copies, waits for them, and re-layouts  17.5 us (14%)
    pallas_call x1, Pallas kernels, body(): pl.pallas_call(functools.partial(kernel, frames, rows_axis), out_shape=ja...  105 us
    unnamed x4, local copies, waits for them, and re-layouts  17.5 us

profile of v1, /device:TPU:8, one launch (start us, length us, event | category | flops | bytes accessed | tf_op | source)
XLA Modules:
  0.0 122.9 jit_solution(10168672097825763924)
XLA Ops:
  0.0 1.4 %copy.8.key_tiles = s32[1,16,9]{2,1,0:T(8,128)} copy(s32[1,16,9]{1,0,2:T(1,128)} %param.12) | data formatting | bytes 1152 | tf_op args[5]
  1.4 6.4 %copy.9.sqkv_hbm = bf16[1152,1728]{1,0:T(8,128)(2,1)} copy(bf16[1152,1728]{0,1:T(8,128)(2,1)} %param.8) | data formatting | bytes 7962624 | tf_op args[1]
  7.8 6.5 %copy.10.tqkv_hbm = bf16[1152,1728]{1,0:T(8,128)(2,1)} copy(bf16[1152,1728]{0,1:T(8,128)(2,1)} %param.10) | data formatting | bytes 7962624 | tf_op args[3]
  14.3 105.4 %shard_map.73 = bf16[16,64,1152]{2,1,0:T(8,128)(2,1)} custom-call(s32[1,16,9]{2,1,0:T(8,128)} %copy.8.key_tiles, s32[1,16]{1,0:T(1,128)} %tile_counts.1, bf16[16,64,1152]{2,1,0:T(8,128)(2,1)} %bitcast.3, bf16[1152,1728]{1,0:T(8,128)(2,1)} %copy.9.sqkv_hbm, bf16[576,1152]{1,0:T(8,128)(2,1)} %sout_hbm.1, bf16[1152,1728]{1,0:T(8,128)(2,1)} %copy.10.tqkv_hbm, ...), custom_call_target="tpu_custom_call" | custom-call | tf_op jit(solution)/shard_map/pallas_call | solution.py:322
  119.6 3.3 %copy.12 = bf16[1,16,64,1152]{3,2,1,0:T(8,128)(2,1)} copy(bf16[1,16,64,1152]{3,2,1,0:T(8,128)(2,1)} %bitcast.2) | data formatting | bytes 4718592

commit v2 on v1

v2 whole, which is shorter than its diff:
```python
import functools
import math

import jax
import jax.numpy as jnp
from jax import lax
from jax.experimental import pallas as pl
from jax.experimental.pallas import tpu as pltpu
from jax.sharding import PartitionSpec as P

HEADS = 8
HD = 72
TH = 4
TW = 16
INNER = HEADS * HD
PADDED = 640
EPS = 1e-06
NEG = -1e30
SCALE = HD ** (-0.5) * math.log2(math.e)
MESH = pl.DeviceIdType.MESH
F32 = jnp.float32
BF16 = jnp.bfloat16
NT = (((1,), (1,)), ((), ()))


def window(head):
    first, last = head * HD, (head + 1) * HD
    low = first // 128 * 128
    high = -(-last // 128) * 128
    return low, high, first - low, last - low


def layer_norm(values):
    centred = values - jnp.mean(values, axis=-1, keepdims=True)
    spread = jnp.mean(centred * centred, axis=-1, keepdims=True)
    return (centred * lax.rsqrt(spread + EPS)).astype(BF16)


def attend(load_q, load_k, load_v, keep, fill):
    columns = [None] * (PADDED // 128)
    for head in range(HEADS):
        low, high, first, last = window(head)
        query = load_q(low, high)
        lane = lax.broadcasted_iota(jnp.int32, query.shape, 1)
        query = jnp.where((lane >= first) & (lane < last), query, jnp.zeros_like(query))
        scores = lax.dot_general(query, load_k(low, high), NT, preferred_element_type=F32)
        scores = jnp.where(keep, scores, fill)
        top = jnp.max(scores, axis=-1, keepdims=True)
        expo = jnp.exp2(scores - top)
        total = jnp.sum(expo, axis=-1, keepdims=True)
        result = jnp.dot(expo.astype(BF16), load_v(low, high), preferred_element_type=F32)
        result = result * (1.0 / total)
        for part in range((high - low) // 128):
            piece = result[:, part * 128 : (part + 1) * 128]
            at = low // 128 + part
            if columns[at] is None:
                columns[at] = piece
            else:
                spot = lax.broadcasted_iota(jnp.int32, piece.shape, 1) + part * 128
                columns[at] = jnp.where(spot >= first, piece, columns[at])
    spot = lax.broadcasted_iota(jnp.int32, columns[-1].shape, 1)
    columns[-1] = jnp.where(spot < INNER - PADDED + 128, columns[-1], 0.0)
    return jnp.concatenate(columns, axis=1)


def kernel(
    frames, rows_axis,
    key_tiles, tile_counts, x_hbm, sqkv_hbm, sout_hbm, tqkv_hbm, tout_hbm, out_hbm,
    xbuf, halo, w_s, w_t, o_s, o_t, qbuf, kbuf, vbuf,
    mixed, landed, heads, rest, tails, back, back_tails, obuf,
    load_sem, halo_send, halo_recv, go_send, go_recv,
    back_send, back_recv, tail_send, tail_recv, store_sem,
):
    frame = lax.axis_index("frame")
    row = lax.axis_index("row")
    above = lax.rem(row + rows_axis - 1, rows_axis)
    below = lax.rem(row + 1, rows_axis)
    feat = x_hbm.shape[-1]
    columns = x_hbm.shape[1]
    slab = TH * columns
    tile_rows = x_hbm.shape[0] // TH
    tile_cols = columns // TW
    tile_len = TH * TW
    group = slab // frames
    half_peers = frames // 2
    parity = lax.rem(frame, 2)
    my_block = parity * half_peers + frame // 2

    barrier = pltpu.get_barrier_semaphore()

    def greet(i, carry):
        pl.semaphore_signal(
            barrier, inc=1, device_id=(lax.rem(frame + i, frames), row), device_id_type=MESH
        )
        return carry

    lax.fori_loop(1, frames, greet, 0)
    for peer in (above, below):
        pl.semaphore_signal(barrier, inc=1, device_id=(frame, peer), device_id_type=MESH)

    def parts(src, dst):
        return [
            (src.at[pl.ds(n * INNER, INNER)], dst.at[pl.ds(n * PADDED, INNER)]) for n in range(3)
        ]

    pairs = [(x_hbm, xbuf)] + parts(sqkv_hbm, w_s) + [(sout_hbm, o_s.at[pl.ds(0, INNER)])]
    pairs += parts(tqkv_hbm, w_t) + [(tout_hbm, o_t.at[pl.ds(0, INNER)])]
    loads = [
        pltpu.make_async_copy(src, dst, load_sem.at[i]) for i, (src, dst) in enumerate(pairs)
    ]
    for load in loads:
        load.start()
    pad_rows = jnp.zeros((PADDED - INNER, feat), BF16)
    for ref in (w_s, w_t):
        for n in range(3):
            ref[n * PADDED + INNER : (n + 1) * PADDED, :] = pad_rows
    o_s[INNER:, :] = pad_rows
    o_t[INNER:, :] = pad_rows

    def tiled(ref, first):
        return jnp.concatenate(
            [
                ref[pl.ds(first, TH), c * TW : (c + 1) * TW, :].reshape(tile_len, feat)
                for c in range(tile_cols)
            ],
            axis=0,
        )

    def project(i, carry):
        normed = layer_norm(tiled(xbuf, i * TH).astype(F32))
        result = lax.dot_general(normed, w_s[...], NT, preferred_element_type=F32)
        qbuf[i] = (result[:, :PADDED] * SCALE).astype(BF16)
        kbuf[i + 1] = result[:, PADDED : 2 * PADDED].astype(BF16)
        vbuf[i + 1] = result[:, 2 * PADDED :].astype(BF16)
        return carry

    def spatial(i):
        rows = tile_rows * row + i
        for half in range(2):
            marks = []
            for c in (2 * half, 2 * half + 1):
                tile = i * tile_cols + c
                count = tile_counts[0, tile]
                spot = lax.broadcasted_iota(jnp.int32, (tile_len, 9 * tile_len), 1) // tile_len
                mark = jnp.zeros((tile_len, 9 * tile_len), jnp.int32)
                for slot in range(key_tiles.shape[0]):
                    target = key_tiles[slot, 0, tile]
                    down = target // tile_cols - rows + 1
                    name = down * 3 + target % tile_cols - half
                    name = jnp.where(slot < count, name, -1)
                    mark = jnp.where(spot == name, 1, mark)
                marks.append(mark)
            keep = jnp.concatenate(marks, axis=0) > 0
            at = half * tile_len
            span = 2 * tile_len

            def load_q(low, high):
                return qbuf[i, 2 * at : 2 * at + span, low:high]

            def load_keys(ref):
                def load(low, high):
                    return jnp.concatenate(
                        [ref[i + d, at : at + 3 * tile_len, low:high] for d in range(3)], axis=0
                    )

                return load

            attended = attend(load_q, load_keys(kbuf), load_keys(vbuf), keep, NEG).astype(BF16)
            branch = jnp.dot(attended, o_s[...], preferred_element_type=F32)
            token = jnp.concatenate(
                [
                    xbuf[pl.ds(i * TH, TH), c * TW : (c + 1) * TW, :].reshape(tile_len, feat)
                    for c in (2 * half, 2 * half + 1)
                ],
                axis=0,
            )
            result = token.astype(F32) + branch
            mixed[i, half * half_peers : (half + 1) * half_peers] = result.reshape(
                half_peers, group, feat
            ).astype(BF16)

            def send(k, carry):
                place = lax.rem(frame // 2 + k, half_peers)
                pltpu.make_async_remote_copy(
                    mixed.at[i, half * half_peers + place], landed.at[i, frame],
                    go_send.at[i], go_recv.at[i],
                    device_id=(2 * place + half, row), device_id_type=MESH,
                ).start()
                return carry

            own = parity if half else 1 - parity
            lax.fori_loop(own, half_peers, send, 0)
        landed[i, frame] = mixed[i, my_block]

    def send_back(src, dst, send_sem, recv_sem):
        def send(k, carry):
            peer = lax.rem(frame + k, frames)
            pltpu.make_async_remote_copy(
                src.at[peer], dst.at[my_block], send_sem, recv_sem,
                device_id=(peer, row), device_id_type=MESH,
            ).start()
            return carry

        dst[my_block] = src[frame]
        lax.fori_loop(1, frames, send, 0)

    def await_all(ref, sem):
        block = ref.at[pl.ds(0, frames - 1)]
        pltpu.make_async_copy(block, block, sem).wait()

    main = PADDED - 128
    left = INNER - main

    def temporal(i, pair, second):
        await_all(landed.at[i], go_recv.at[i])
        normed = layer_norm(landed[i].astype(F32).reshape(slab, feat))
        result = lax.dot_general(normed, w_t[...], NT, preferred_element_type=F32)
        queries = (result[:, :PADDED] * SCALE).astype(BF16)
        key_vecs = result[:, PADDED : 2 * PADDED].astype(BF16)
        val_vecs = result[:, 2 * PADDED :].astype(BF16)
        mine = lax.broadcasted_iota(jnp.int32, (slab, slab), 0) % group
        theirs = lax.broadcasted_iota(jnp.int32, (slab, slab), 1) % group
        attended = attend(
            lambda low, high: queries[:, low:high],
            lambda low, high: key_vecs[:, low:high],
            lambda low, high: val_vecs[:, low:high],
            mine == theirs,
            -jnp.inf,
        )
        heads[i] = attended[:, :main].reshape(frames, group, main).astype(BF16)
        send_back(heads.at[i], back.at[i], back_send.at[i], back_recv.at[i])
        if second:
            lane = lax.broadcasted_iota(jnp.int32, (slab, 128), 1)
            both = jnp.where(lane < left, rest[...], pltpu.roll(attended[:, main:], left, 1))
            tails[pair] = both.reshape(frames, group, 128).astype(BF16)
            send_back(tails.at[pair], back_tails.at[pair], tail_send.at[pair], tail_recv.at[pair])
        else:
            rest[...] = attended[:, main:]

    def finish(i, pair, second):
        await_all(back.at[i], back_recv.at[i])
        if not second:
            await_all(back_tails.at[pair], tail_recv.at[pair])
        tail = back_tails[pair].astype(F32).reshape(slab, 128)
        if second:
            tail = pltpu.roll(tail, left, 1)
        attended = jnp.concatenate([back[i].astype(F32).reshape(slab, main), tail], axis=1)
        branch = jnp.dot(attended.astype(BF16), o_t[...], preferred_element_type=F32)
        result = (mixed[i].astype(F32).reshape(slab, feat) + branch).astype(BF16)
        for c in range(tile_cols):
            obuf[pl.ds(i * TH, TH), c * TW : (c + 1) * TW, :] = result[
                c * tile_len : (c + 1) * tile_len
            ].reshape(TH, TW, feat)
        pltpu.make_async_copy(
            obuf.at[pl.ds(i * TH, TH)], out_hbm.at[pl.ds(i * TH, TH)], store_sem.at[i]
        ).start()

    for load in loads[:4]:
        load.wait()
    lax.fori_loop(0, 2, project, 0)
    loads[4].wait()

    pl.semaphore_wait(barrier, frames + 1)
    send_down = pltpu.make_async_remote_copy(
        x_hbm.at[pl.ds((tile_rows - 1) * TH, TH)], halo.at[0], halo_send.at[0], halo_recv.at[0],
        device_id=(frame, below), device_id_type=MESH,
    )
    send_up = pltpu.make_async_remote_copy(
        x_hbm.at[pl.ds(0, TH)], halo.at[1], halo_send.at[1], halo_recv.at[1],
        device_id=(frame, above), device_id_type=MESH,
    )
    send_down.start()
    send_up.start()

    def inner_rows(n, carry):
        project(n + 1, 0)
        spatial(n)
        return carry

    lax.fori_loop(1, tile_rows - 1, inner_rows, 0)

    send_down.wait()
    send_up.wait()

    def project_halo(n, carry):
        normed = layer_norm(tiled(halo.at[n], 0).astype(F32))
        result = lax.dot_general(normed, w_s[PADDED:, :], NT, preferred_element_type=F32)
        place = n * (tile_rows + 1)
        kbuf[place] = result[:, :PADDED].astype(BF16)
        vbuf[place] = result[:, PADDED:].astype(BF16)
        return carry

    lax.fori_loop(0, 2, project_halo, 0)

    def outer_rows(n, carry):
        spatial(n * (tile_rows - 1))
        return carry

    lax.fori_loop(0, 2, outer_rows, 0)

    for load in loads[5:]:
        load.wait()

    def in_order(step):
        def run(pair, carry):
            for second in range(2):
                step((1 - pair) + second * (1 + (tile_rows - 2) * pair), pair, bool(second))
            return carry

        lax.fori_loop(0, 2, run, 0)

    in_order(temporal)
    in_order(finish)

    for i in range(tile_rows):
        await_all(landed.at[i], go_send.at[i])
        await_all(back.at[i], back_send.at[i])
        pltpu.make_async_copy(
            obuf.at[pl.ds(i * TH, TH)], out_hbm.at[pl.ds(i * TH, TH)], store_sem.at[i]
        ).wait()
    for pair in range(2):
        await_all(back_tails.at[pair], tail_send.at[pair])


def body(frames_in, spatial_qkv, spatial_out, temporal_qkv, temporal_out, key_tiles, tile_counts):
    frames = lax.axis_size("frame")
    rows_axis = lax.axis_size("row")
    rows, columns, feat = frames_in.shape[1:]
    slab = TH * columns
    tile_rows = rows // TH
    group = slab // frames
    dma = pltpu.SemaphoreType.DMA
    smem = pl.BlockSpec(memory_space=pltpu.SMEM)
    hbm = pl.BlockSpec(memory_space=pl.ANY)
    result = pl.pallas_call(
        functools.partial(kernel, frames, rows_axis),
        out_shape=jax.ShapeDtypeStruct((rows, columns, feat), BF16),
        in_specs=[smem, smem, hbm, hbm, hbm, hbm, hbm],
        out_specs=hbm,
        scratch_shapes=[
            pltpu.VMEM((rows, columns, feat), BF16),
            pltpu.VMEM((2, TH, columns, feat), BF16),
            pltpu.VMEM((3 * PADDED, feat), BF16),
            pltpu.VMEM((3 * PADDED, feat), BF16),
            pltpu.VMEM((PADDED, feat), BF16),
            pltpu.VMEM((PADDED, feat), BF16),
            pltpu.VMEM((tile_rows, slab, PADDED), BF16),
            pltpu.VMEM((tile_rows + 2, slab, PADDED), BF16),
            pltpu.VMEM((tile_rows + 2, slab, PADDED), BF16),
            pltpu.VMEM((tile_rows, frames, group, feat), BF16),
            pltpu.VMEM((tile_rows, frames, group, feat), BF16),
            pltpu.VMEM((tile_rows, frames, group, PADDED - 128), BF16),
            pltpu.VMEM((slab, 128), F32),
            pltpu.VMEM((2, frames, group, 128), BF16),
            pltpu.VMEM((tile_rows, frames, group, PADDED - 128), BF16),
            pltpu.VMEM((2, frames, group, 128), BF16),
            pltpu.VMEM((rows, columns, feat), BF16),
            dma((9,)),
            dma((2,)),
            dma((2,)),
            dma((tile_rows,)),
            dma((tile_rows,)),
            dma((tile_rows,)),
            dma((tile_rows,)),
            dma((2,)),
            dma((2,)),
            dma((tile_rows,)),
        ],
        compiler_params=pltpu.CompilerParams(
            collective_id=0, has_side_effects=True, vmem_limit_bytes=67043328
        ),
    )(
        jnp.transpose(key_tiles, (2, 0, 1)), tile_counts, frames_in[0],
        spatial_qkv.T, spatial_out, temporal_qkv.T, temporal_out,
    )
    return result[None]


def solution(mesh):
    in_specs = (
        P("frame", "row", None, None),
        P(),
        P(),
        P(),
        P(),
        P("frame", "row", None),
        P("frame", "row"),
    )
    out_specs = P("frame", "row", None, None)
    return jax.shard_map(body, mesh=mesh, in_specs=in_specs, out_specs=out_specs, check_vma=False)
```

time: 123 us -> 103 us (0.84)
  local copies, waits for them, and re-layouts: 17.5 us -> 3.26 us
  Pallas kernels: 105 us -> 100 us
    unnamed x4 -> x1, local copies, waits for them, and re-layouts: 17.5 us -> 3.26 us
    pallas_call x1, Pallas kernels: 105 us -> 100 us  [body(): pl.pallas_call(functools.partial(kernel, frames, rows_axis), out_shape=ja...]
where the time goes in v2:
time: 103 us
  Pallas kernels  100 us (97%)
  local copies, waits for them, and re-layouts  3.26 us (3%)
    pallas_call x1, Pallas kernels, body(): pl.pallas_call(functools.partial(kernel, frames, rows_axis), out_shape=ja...  100 us
    unnamed x1, local copies, waits for them, and re-layouts  3.26 us

profile of v2, /device:TPU:8, one launch (start us, length us, event | category | flops | bytes accessed | tf_op | source)
XLA Modules:
  0.0 103.3 jit_solution(12249703773511826571)
XLA Ops:
  0.0 100.0 %shard_map.73 = bf16[16,64,1152]{2,1,0:T(8,128)(2,1)} custom-call(s32[9,1,16]{2,1,0:T(1,128)} %bitcast.9, s32[1,16]{1,0:T(1,128)} %tile_counts.1, bf16[16,64,1152]{2,1,0:T(8,128)(2,1)} %bitcast.8, bf16[1728,1152]{1,0:T(8,128)(2,1)} %bitcast.6, bf16[576,1152]{1,0:T(8,128)(2,1)} %sout_hbm.1, bf16[1728,1152]{1,0:T(8,128)(2,1)} %bitcast.7, ...), custom_call_target="tpu_custom_call" | custom-call | tf_op jit(solution)/shard_map/pallas_call | solution.py:335
  100.0 3.3 %copy.9 = bf16[1,16,64,1152]{3,2,1,0:T(8,128)(2,1)} copy(bf16[1,16,64,1152]{3,2,1,0:T(8,128)(2,1)} %bitcast.5) | data formatting | bytes 4718592

commit v3 on v2

--- a/solution.py
+++ b/solution.py
@@ -65,10 +65,10 @@
 
 def kernel(
     frames, rows_axis,
-    key_tiles, tile_counts, x_hbm, sqkv_hbm, sout_hbm, tqkv_hbm, tout_hbm, out_hbm,
-    xbuf, halo, w_s, w_t, o_s, o_t, qbuf, kbuf, vbuf,
+    tiles_hbm, counts_hbm, x_hbm, sqkv_hbm, sout_hbm, tqkv_hbm, tout_hbm, out_hbm,
+    key_tiles, tile_counts, xbuf, halo, w_s, w_t, o_s, o_t, qbuf, kbuf, vbuf,
     mixed, landed, heads, rest, tails, back, back_tails, obuf,
-    load_sem, halo_send, halo_recv, go_send, go_recv,
+    load_sem, x_sem, halo_send, halo_recv, go_send, go_recv,
     back_send, back_recv, tail_send, tail_recv, store_sem,
 ):
     frame = lax.axis_index("frame")
@@ -103,12 +103,22 @@
             (src.at[pl.ds(n * INNER, INNER)], dst.at[pl.ds(n * PADDED, INNER)]) for n in range(3)
         ]
 
-    pairs = [(x_hbm, xbuf)] + parts(sqkv_hbm, w_s) + [(sout_hbm, o_s.at[pl.ds(0, INNER)])]
+    def load_rows(i):
+        block = pl.ds(i * TH, TH)
+        return pltpu.make_async_copy(x_hbm.at[block], xbuf.at[block], x_sem.at[i])
+
+    pairs = parts(sqkv_hbm, w_s) + [(sout_hbm, o_s.at[pl.ds(0, INNER)])]
+    pairs += [(tiles_hbm, key_tiles), (counts_hbm, tile_counts)]
     pairs += parts(tqkv_hbm, w_t) + [(tout_hbm, o_t.at[pl.ds(0, INNER)])]
     loads = [
         pltpu.make_async_copy(src, dst, load_sem.at[i]) for i, (src, dst) in enumerate(pairs)
     ]
-    for load in loads:
+    load_rows(0).start()
+    for load in loads[:3]:
+        load.start()
+    for i in range(1, tile_rows):
+        load_rows(i).start()
+    for load in loads[3:]:
         load.start()
     pad_rows = jnp.zeros((PADDED - INNER, feat), BF16)
     for ref in (w_s, w_t):
@@ -126,15 +136,18 @@
             axis=0,
         )
 
-    def project(i, carry):
+    def project_queries(i):
         normed = layer_norm(tiled(xbuf, i * TH).astype(F32))
-        result = lax.dot_general(normed, w_s[...], NT, preferred_element_type=F32)
-        qbuf[i] = (result[:, :PADDED] * SCALE).astype(BF16)
-        kbuf[i + 1] = result[:, PADDED : 2 * PADDED].astype(BF16)
-        vbuf[i + 1] = result[:, 2 * PADDED :].astype(BF16)
-        return carry
-
-    def spatial(i):
+        result = lax.dot_general(normed, w_s[:PADDED, :], NT, preferred_element_type=F32)
+        qbuf[i] = (result * SCALE).astype(BF16)
+
+    def project_keys(ref, first, place):
+        normed = layer_norm(tiled(ref, first).astype(F32))
+        result = lax.dot_general(normed, w_s[PADDED:, :], NT, preferred_element_type=F32)
+        kbuf[place] = result[:, :PADDED].astype(BF16)
+        vbuf[place] = result[:, PADDED:].astype(BF16)
+
+    def spatial(i, before_send):
         rows = tile_rows * row + i
         for half in range(2):
             marks = []
@@ -179,6 +192,9 @@
                 half_peers, group, feat
             ).astype(BF16)
 
+            if half == 0:
+                before_send()
+
             def send(k, carry):
                 place = lax.rem(frame // 2 + k, half_peers)
                 pltpu.make_async_remote_copy(
@@ -228,14 +244,18 @@
             -jnp.inf,
         )
         heads[i] = attended[:, :main].reshape(frames, group, main).astype(BF16)
-        send_back(heads.at[i], back.at[i], back_send.at[i], back_recv.at[i])
         if second:
             lane = lax.broadcasted_iota(jnp.int32, (slab, 128), 1)
             both = jnp.where(lane < left, rest[...], pltpu.roll(attended[:, main:], left, 1))
             tails[pair] = both.reshape(frames, group, 128).astype(BF16)
-            send_back(tails.at[pair], back_tails.at[pair], tail_send.at[pair], tail_recv.at[pair])
         else:
             rest[...] = attended[:, main:]
+
+    def send_heads(i):
+        send_back(heads.at[i], back.at[i], back_send.at[i], back_recv.at[i])
+
+    def send_tails(pair):
+        send_back(tails.at[pair], back_tails.at[pair], tail_send.at[pair], tail_recv.at[pair])
 
     def finish(i, pair, second):
         await_all(back.at[i], back_recv.at[i])
@@ -255,65 +275,94 @@
             obuf.at[pl.ds(i * TH, TH)], out_hbm.at[pl.ds(i * TH, TH)], store_sem.at[i]
         ).start()
 
-    for load in loads[:4]:
+    load_rows(0).wait()
+    for load in loads[:3]:
         load.wait()
-    lax.fori_loop(0, 2, project, 0)
-    loads[4].wait()
-
-    pl.semaphore_wait(barrier, frames + 1)
+    last = tile_rows - 1
+
+    def first_keys(i, carry):
+        @pl.when(i > 0)
+        def _():
+            load_rows(i).wait()
+
+        project_keys(xbuf, i * TH, i + 1)
+        return carry
+
+    lax.fori_loop(0, last, first_keys, 0)
+    project_queries(1)
+    for load in loads[3:6]:
+        load.wait()
+
     send_down = pltpu.make_async_remote_copy(
-        x_hbm.at[pl.ds((tile_rows - 1) * TH, TH)], halo.at[0], halo_send.at[0], halo_recv.at[0],
+        x_hbm.at[pl.ds(last * TH, TH)], halo.at[0], halo_send.at[0], halo_recv.at[0],
         device_id=(frame, below), device_id_type=MESH,
     )
     send_up = pltpu.make_async_remote_copy(
         x_hbm.at[pl.ds(0, TH)], halo.at[1], halo_send.at[1], halo_recv.at[1],
         device_id=(frame, above), device_id_type=MESH,
     )
-    send_down.start()
-    send_up.start()
-
-    def inner_rows(n, carry):
-        project(n + 1, 0)
-        spatial(n)
+
+    def meet():
+        pl.semaphore_wait(barrier, frames + 1)
+        send_down.start()
+        send_up.start()
+
+    spatial(1, meet)
+    load_rows(last).wait()
+    project_keys(xbuf, last * TH, tile_rows)
+
+    def other_rows(n, carry):
+        @pl.when(n == 1)
+        def _():
+            send_down.wait()
+            send_up.wait()
+
+            def halo_keys(k, carry):
+                project_keys(halo.at[k], 0, k * (tile_rows + 1))
+                return carry
+
+            lax.fori_loop(0, 2, halo_keys, 0)
+
+        i = jnp.where(n == 0, 2, (n - 1) * last)
+        project_queries(i)
+        spatial(i, lambda: None)
         return carry
 
-    lax.fori_loop(1, tile_rows - 1, inner_rows, 0)
-
-    send_down.wait()
-    send_up.wait()
-
-    def project_halo(n, carry):
-        normed = layer_norm(tiled(halo.at[n], 0).astype(F32))
-        result = lax.dot_general(normed, w_s[PADDED:, :], NT, preferred_element_type=F32)
-        place = n * (tile_rows + 1)
-        kbuf[place] = result[:, :PADDED].astype(BF16)
-        vbuf[place] = result[:, PADDED:].astype(BF16)
+    lax.fori_loop(0, last, other_rows, 0)
+
+    for load in loads[6:]:
+        load.wait()
+
+    def place_of(pair, second):
+        return (1 - pair) + second * (1 + (tile_rows - 2) * pair)
+
+    def temporal_pair(pair, carry):
+        temporal(place_of(pair, 0), pair, False)
+
+        @pl.when(pair == 1)
+        def _():
+            for i in range(tile_rows):
+                await_all(landed.at[i], go_send.at[i])
+            send_heads(1)
+            send_heads(2)
+            send_tails(0)
+            send_heads(0)
+
+        temporal(place_of(pair, 1), pair, True)
         return carry
 
-    lax.fori_loop(0, 2, project_halo, 0)
-
-    def outer_rows(n, carry):
-        spatial(n * (tile_rows - 1))
+    lax.fori_loop(0, 2, temporal_pair, 0)
+    send_heads(last)
+    send_tails(1)
+
+    def finish_pair(pair, carry):
+        for second in range(2):
+            finish(place_of(pair, second), pair, bool(second))
         return carry
 
-    lax.fori_loop(0, 2, outer_rows, 0)
-
-    for load in loads[5:]:
-        load.wait()
-
-    def in_order(step):
-        def run(pair, carry):
-            for second in range(2):
-                step((1 - pair) + second * (1 + (tile_rows - 2) * pair), pair, bool(second))
-            return carry
-
-        lax.fori_loop(0, 2, run, 0)
-
-    in_order(temporal)
-    in_order(finish)
+    lax.fori_loop(0, 2, finish_pair, 0)
 
     for i in range(tile_rows):
-        await_all(landed.at[i], go_send.at[i])
         await_all(back.at[i], back_send.at[i])
         pltpu.make_async_copy(
             obuf.at[pl.ds(i * TH, TH)], out_hbm.at[pl.ds(i * TH, TH)], store_sem.at[i]
@@ -330,14 +379,15 @@
     tile_rows = rows // TH
     group = slab // frames
     dma = pltpu.SemaphoreType.DMA
-    smem = pl.BlockSpec(memory_space=pltpu.SMEM)
-    hbm = pl.BlockSpec(memory_space=pl.ANY)
+    hbm = pl.BlockSpec(memory_space=pltpu.HBM)
     result = pl.pallas_call(
         functools.partial(kernel, frames, rows_axis),
         out_shape=jax.ShapeDtypeStruct((rows, columns, feat), BF16),
-        in_specs=[smem, smem, hbm, hbm, hbm, hbm, hbm],
-        out_specs=hbm,
+        in_specs=[hbm] * 7,
+        out_specs=pl.BlockSpec(memory_space=pl.ANY),
         scratch_shapes=[
+            pltpu.SMEM(key_tiles.shape[2:] + (1, key_tiles.shape[1]), jnp.int32),
+            pltpu.SMEM(tile_counts.shape, jnp.int32),
             pltpu.VMEM((rows, columns, feat), BF16),
             pltpu.VMEM((2, TH, columns, feat), BF16),
             pltpu.VMEM((3 * PADDED, feat), BF16),
@@ -355,7 +405,8 @@
             pltpu.VMEM((tile_rows, frames, group, PADDED - 128), BF16),
             pltpu.VMEM((2, frames, group, 128), BF16),
             pltpu.VMEM((rows, columns, feat), BF16),
-            dma((9,)),
+            dma((10,)),
+            dma((tile_rows,)),
             dma((2,)),
             dma((2,)),
             dma((tile_rows,)),
@@ -367,11 +418,16 @@
             dma((tile_rows,)),
         ],
         compiler_params=pltpu.CompilerParams(
-            collective_id=0, has_side_effects=True, vmem_limit_bytes=67043328
+            collective_id=0, has_side_effects=True, vmem_limit_bytes=44 * 2**20
         ),
     )(
-        jnp.transpose(key_tiles, (2, 0, 1)), tile_counts, frames_in[0],
-        spatial_qkv.T, spatial_out, temporal_qkv.T, temporal_out,
+        *(
+            pltpu.with_memory_space_constraint(array, pltpu.HBM)
+            for array in (
+                jnp.transpose(key_tiles, (2, 0, 1)), tile_counts, frames_in[0],
+                spatial_qkv.T, spatial_out, temporal_qkv.T, temporal_out,
+            )
+        )
     )
     return result[None]
 

time: 103 us -> 100 us (0.971)
  local copies, waits for them, and re-layouts: 3.26 us -> 1.41 us
  Pallas kernels: 100 us -> 98.6 us
    unnamed x1, local copies, waits for them, and re-layouts: 3.26 us -> 1.41 us
    pallas_call x1, Pallas kernels: 100 us -> 98.6 us  [body(): pl.pallas_call(functools.partial(kernel, frames, rows_axis), out_shape=ja...]
where the time goes in v3:
time: 100 us
  Pallas kernels  98.6 us (99%)
  local copies, waits for them, and re-layouts  1.41 us (1%)
    pallas_call x1, Pallas kernels, body(): pl.pallas_call(functools.partial(kernel, frames, rows_axis), out_shape=ja...  98.6 us

profile of v3, /device:TPU:8, one launch (start us, length us, event | category | flops | bytes accessed | tf_op | source)
XLA Modules:
  0.0 100.0 jit_solution(9685385953383156794)
XLA Ops:
  0.0 98.6 %shard_map.73 = bf16[16,64,1152]{2,1,0:T(8,128)(2,1)S(1)} custom-call(s32[9,1,16]{2,1,0:T(1,128)} %bitcast.9, s32[1,16]{1,0:T(1,128)} %counts_hbm.1, bf16[16,64,1152]{2,1,0:T(8,128)(2,1)} %bitcast.8, bf16[1728,1152]{1,0:T(8,128)(2,1)} %bitcast.6, bf16[576,1152]{1,0:T(8,128)(2,1)} %sout_hbm.1, bf16[1728,1152]{1,0:T(8,128)(2,1)} %bitcast.7, ...), custom_call_target="tpu_custom_call" | custom-call | tf_op jit(solution)/shard_map/pallas_call | solution.py:383
  98.6 1.4 %copy.9 = bf16[1,16,64,1152]{3,2,1,0:T(8,128)(2,1)} copy(bf16[1,16,64,1152]{3,2,1,0:T(8,128)(2,1)S(1)} %bitcast.5) | data formatting | bytes 4718592

commit v4 on v3

--- a/solution.py
+++ b/solution.py
@@ -67,9 +67,9 @@
     frames, rows_axis,
     tiles_hbm, counts_hbm, x_hbm, sqkv_hbm, sout_hbm, tqkv_hbm, tout_hbm, out_hbm,
     key_tiles, tile_counts, xbuf, halo, w_s, w_t, o_s, o_t, qbuf, kbuf, vbuf,
-    mixed, landed, heads, rest, tails, back, back_tails, obuf,
+    mixed, landed, heads, long_heads, rest, back, long_back, obuf,
     load_sem, x_sem, halo_send, halo_recv, go_send, go_recv,
-    back_send, back_recv, tail_send, tail_recv, store_sem,
+    back_send, back_recv, long_send, long_recv, store_sem,
 ):
     frame = lax.axis_index("frame")
     row = lax.axis_index("row")
@@ -100,7 +100,7 @@
 
     def parts(src, dst):
         return [
-            (src.at[pl.ds(n * INNER, INNER)], dst.at[pl.ds(n * PADDED, INNER)]) for n in range(3)
+            (src.at[pl.ds(n * INNER, INNER)], dst.at[pl.ds(n * PADDED, INNER)]) for n in (1, 2, 0)
         ]
 
     def load_rows(i):
@@ -114,11 +114,14 @@
         pltpu.make_async_copy(src, dst, load_sem.at[i]) for i, (src, dst) in enumerate(pairs)
     ]
     load_rows(0).start()
-    for load in loads[:3]:
+    for load in loads[:2]:
         load.start()
-    for i in range(1, tile_rows):
+    for i in range(1, tile_rows - 1):
         load_rows(i).start()
-    for load in loads[3:]:
+    for load in loads[2:6]:
+        load.start()
+    load_rows(tile_rows - 1).start()
+    for load in loads[6:]:
         load.start()
     pad_rows = jnp.zeros((PADDED - INNER, feat), BF16)
     for ref in (w_s, w_t):
@@ -127,19 +130,19 @@
     o_s[INNER:, :] = pad_rows
     o_t[INNER:, :] = pad_rows
 
-    def tiled(ref, first):
+    def tiled(ref, first, low=0, high=tile_cols):
         return jnp.concatenate(
             [
                 ref[pl.ds(first, TH), c * TW : (c + 1) * TW, :].reshape(tile_len, feat)
-                for c in range(tile_cols)
+                for c in range(low, high)
             ],
             axis=0,
         )
 
-    def project_queries(i):
-        normed = layer_norm(tiled(xbuf, i * TH).astype(F32))
+    def project_queries(i, low=0, high=tile_cols):
+        normed = layer_norm(tiled(xbuf, i * TH, low, high).astype(F32))
         result = lax.dot_general(normed, w_s[:PADDED, :], NT, preferred_element_type=F32)
-        qbuf[i] = (result * SCALE).astype(BF16)
+        qbuf[i, low * tile_len : high * tile_len] = (result * SCALE).astype(BF16)
 
     def project_keys(ref, first, place):
         normed = layer_norm(tiled(ref, first).astype(F32))
@@ -147,9 +150,10 @@
         kbuf[place] = result[:, :PADDED].astype(BF16)
         vbuf[place] = result[:, PADDED:].astype(BF16)
 
-    def spatial(i, before_send):
+    def spatial(i, before_half, before_send):
         rows = tile_rows * row + i
         for half in range(2):
+            before_half(half)
             marks = []
             for c in (2 * half, 2 * half + 1):
                 tile = i * tile_cols + c
@@ -180,13 +184,7 @@
 
             attended = attend(load_q, load_keys(kbuf), load_keys(vbuf), keep, NEG).astype(BF16)
             branch = jnp.dot(attended, o_s[...], preferred_element_type=F32)
-            token = jnp.concatenate(
-                [
-                    xbuf[pl.ds(i * TH, TH), c * TW : (c + 1) * TW, :].reshape(tile_len, feat)
-                    for c in (2 * half, 2 * half + 1)
-                ],
-                axis=0,
-            )
+            token = tiled(xbuf, i * TH, 2 * half, 2 * half + 2)
             result = token.astype(F32) + branch
             mixed[i, half * half_peers : (half + 1) * half_peers] = result.reshape(
                 half_peers, group, feat
@@ -243,28 +241,34 @@
             mine == theirs,
             -jnp.inf,
         )
-        heads[i] = attended[:, :main].reshape(frames, group, main).astype(BF16)
         if second:
             lane = lax.broadcasted_iota(jnp.int32, (slab, 128), 1)
             both = jnp.where(lane < left, rest[...], pltpu.roll(attended[:, main:], left, 1))
-            tails[pair] = both.reshape(frames, group, 128).astype(BF16)
+            whole = jnp.concatenate([attended[:, :main], both], axis=1)
+            long_heads[pair] = whole.reshape(frames, group, PADDED).astype(BF16)
         else:
+            heads[pair] = attended[:, :main].reshape(frames, group, main).astype(BF16)
             rest[...] = attended[:, main:]
 
-    def send_heads(i):
-        send_back(heads.at[i], back.at[i], back_send.at[i], back_recv.at[i])
-
-    def send_tails(pair):
-        send_back(tails.at[pair], back_tails.at[pair], tail_send.at[pair], tail_recv.at[pair])
+    def send_first(pair):
+        send_back(heads.at[pair], back.at[pair], back_send.at[pair], back_recv.at[pair])
+
+    def send_second(pair):
+        send_back(
+            long_heads.at[pair], long_back.at[pair], long_send.at[pair], long_recv.at[pair]
+        )
 
     def finish(i, pair, second):
-        await_all(back.at[i], back_recv.at[i])
-        if not second:
-            await_all(back_tails.at[pair], tail_recv.at[pair])
-        tail = back_tails[pair].astype(F32).reshape(slab, 128)
         if second:
-            tail = pltpu.roll(tail, left, 1)
-        attended = jnp.concatenate([back[i].astype(F32).reshape(slab, main), tail], axis=1)
+            long = long_back[pair].astype(F32).reshape(slab, PADDED)
+            part = long[:, :main]
+            tail = pltpu.roll(long[:, main:], left, 1)
+        else:
+            await_all(back.at[pair], back_recv.at[pair])
+            await_all(long_back.at[pair], long_recv.at[pair])
+            part = back[pair].astype(F32).reshape(slab, main)
+            tail = long_back[pair, :, :, main:].astype(F32).reshape(slab, 128)
+        attended = jnp.concatenate([part, tail], axis=1)
         branch = jnp.dot(attended.astype(BF16), o_t[...], preferred_element_type=F32)
         result = (mixed[i].astype(F32).reshape(slab, feat) + branch).astype(BF16)
         for c in range(tile_cols):
@@ -276,7 +280,7 @@
         ).start()
 
     load_rows(0).wait()
-    for load in loads[:3]:
+    for load in loads[:2]:
         load.wait()
     last = tile_rows - 1
 
@@ -289,8 +293,7 @@
         return carry
 
     lax.fori_loop(0, last, first_keys, 0)
-    project_queries(1)
-    for load in loads[3:6]:
+    for load in loads[2:6]:
         load.wait()
 
     send_down = pltpu.make_async_remote_copy(
@@ -307,7 +310,7 @@
         send_down.start()
         send_up.start()
 
-    spatial(1, meet)
+    spatial(1, lambda half: project_queries(1, 2 * half, 2 * half + 2), meet)
     load_rows(last).wait()
     project_keys(xbuf, last * TH, tile_rows)
 
@@ -325,7 +328,7 @@
 
         i = jnp.where(n == 0, 2, (n - 1) * last)
         project_queries(i)
-        spatial(i, lambda: None)
+        spatial(i, lambda half: None, lambda: None)
         return carry
 
     lax.fori_loop(0, last, other_rows, 0)
@@ -343,17 +346,15 @@
         def _():
             for i in range(tile_rows):
                 await_all(landed.at[i], go_send.at[i])
-            send_heads(1)
-            send_heads(2)
-            send_tails(0)
-            send_heads(0)
+            send_first(0)
+            send_second(0)
+            send_first(1)
 
         temporal(place_of(pair, 1), pair, True)
         return carry
 
     lax.fori_loop(0, 2, temporal_pair, 0)
-    send_heads(last)
-    send_tails(1)
+    send_second(1)
 
     def finish_pair(pair, carry):
         for second in range(2):
@@ -362,13 +363,13 @@
 
     lax.fori_loop(0, 2, finish_pair, 0)
 
+    for pair in range(2):
+        await_all(back.at[pair], back_send.at[pair])
+        await_all(long_back.at[pair], long_send.at[pair])
     for i in range(tile_rows):
-        await_all(back.at[i], back_send.at[i])
         pltpu.make_async_copy(
             obuf.at[pl.ds(i * TH, TH)], out_hbm.at[pl.ds(i * TH, TH)], store_sem.at[i]
         ).wait()
-    for pair in range(2):
-        await_all(back_tails.at[pair], tail_send.at[pair])
 
 
 def body(frames_in, spatial_qkv, spatial_out, temporal_qkv, temporal_out, key_tiles, tile_counts):
@@ -399,11 +400,11 @@
             pltpu.VMEM((tile_rows + 2, slab, PADDED), BF16),
             pltpu.VMEM((tile_rows, frames, group, feat), BF16),
             pltpu.VMEM((tile_rows, frames, group, feat), BF16),
-            pltpu.VMEM((tile_rows, frames, group, PADDED - 128), BF16),
+            pltpu.VMEM((2, frames, group, PADDED - 128), BF16),
+            pltpu.VMEM((2, frames, group, PADDED), BF16),
             pltpu.VMEM((slab, 128), F32),
-            pltpu.VMEM((2, frames, group, 128), BF16),
-            pltpu.VMEM((tile_rows, frames, group, PADDED - 128), BF16),
-            pltpu.VMEM((2, frames, group, 128), BF16),
+            pltpu.VMEM((2, frames, group, PADDED - 128), BF16),
+            pltpu.VMEM((2, frames, group, PADDED), BF16),
             pltpu.VMEM((rows, columns, feat), BF16),
             dma((10,)),
             dma((tile_rows,)),
@@ -411,8 +412,8 @@
             dma((2,)),
             dma((tile_rows,)),
             dma((tile_rows,)),
-            dma((tile_rows,)),
-            dma((tile_rows,)),
+            dma((2,)),
+            dma((2,)),
             dma((2,)),
             dma((2,)),
             dma((tile_rows,)),

time: 100 us -> 99 us (0.990)
  Pallas kernels: 98.6 us -> 97.5 us
    pallas_call x1, Pallas kernels: 98.6 us -> 97.5 us  [body(): pl.pallas_call(functools.partial(kernel, frames, rows_axis), out_shape=ja...]
where the time goes in v4:
time: 99 us
  Pallas kernels  97.5 us (98%)
  local copies, waits for them, and re-layouts  1.41 us (1%)
    pallas_call x1, Pallas kernels, body(): pl.pallas_call(functools.partial(kernel, frames, rows_axis), out_shape=ja...  97.5 us

profile of v4, /device:TPU:8, one launch (start us, length us, event | category | flops | bytes accessed | tf_op | source)
XLA Modules:
  0.0 99.0 jit_solution(13053486920944170156)
XLA Ops:
  0.0 97.5 %shard_map.73 = bf16[16,64,1152]{2,1,0:T(8,128)(2,1)S(1)} custom-call(s32[9,1,16]{2,1,0:T(1,128)} %bitcast.9, s32[1,16]{1,0:T(1,128)} %counts_hbm.1, bf16[16,64,1152]{2,1,0:T(8,128)(2,1)} %bitcast.8, bf16[1728,1152]{1,0:T(8,128)(2,1)} %bitcast.6, bf16[576,1152]{1,0:T(8,128)(2,1)} %sout_hbm.1, bf16[1728,1152]{1,0:T(8,128)(2,1)} %bitcast.7, ...), custom_call_target="tpu_custom_call" | custom-call | tf_op jit(solution)/shard_map/pallas_call | solution.py:384
  97.6 1.4 %copy.9 = bf16[1,16,64,1152]{3,2,1,0:T(8,128)(2,1)} copy(bf16[1,16,64,1152]{3,2,1,0:T(8,128)(2,1)S(1)} %bitcast.5) | data formatting | bytes 4718592

commit v5 on v4

--- a/solution.py
+++ b/solution.py
@@ -113,12 +113,9 @@
     loads = [
         pltpu.make_async_copy(src, dst, load_sem.at[i]) for i, (src, dst) in enumerate(pairs)
     ]
-    load_rows(0).start()
-    for load in loads[:2]:
-        load.start()
-    for i in range(1, tile_rows - 1):
+    for i in range(tile_rows - 1):
         load_rows(i).start()
-    for load in loads[2:6]:
+    for load in loads[:6]:
         load.start()
     load_rows(tile_rows - 1).start()
     for load in loads[6:]:
@@ -139,10 +136,10 @@
             axis=0,
         )
 
-    def project_queries(i, low=0, high=tile_cols):
-        normed = layer_norm(tiled(xbuf, i * TH, low, high).astype(F32))
+    def project_queries(i):
+        normed = layer_norm(tiled(xbuf, i * TH).astype(F32))
         result = lax.dot_general(normed, w_s[:PADDED, :], NT, preferred_element_type=F32)
-        qbuf[i, low * tile_len : high * tile_len] = (result * SCALE).astype(BF16)
+        qbuf[i] = (result * SCALE).astype(BF16)
 
     def project_keys(ref, first, place):
         normed = layer_norm(tiled(ref, first).astype(F32))
@@ -150,10 +147,9 @@
         kbuf[place] = result[:, :PADDED].astype(BF16)
         vbuf[place] = result[:, PADDED:].astype(BF16)
 
-    def spatial(i, before_half, before_send):
+    def spatial(i, before_send):
         rows = tile_rows * row + i
         for half in range(2):
-            before_half(half)
             marks = []
             for c in (2 * half, 2 * half + 1):
                 tile = i * tile_cols + c
@@ -279,22 +275,31 @@
             obuf.at[pl.ds(i * TH, TH)], out_hbm.at[pl.ds(i * TH, TH)], store_sem.at[i]
         ).start()
 
-    load_rows(0).wait()
+    last = tile_rows - 1
+
+    def norm_first(i, carry):
+        load_rows(i).wait()
+        normed = layer_norm(tiled(xbuf, i * TH).astype(F32))
+        obuf[pl.ds(i * TH, TH)] = normed.reshape(TH, columns, feat)
+        return carry
+
+    lax.fori_loop(0, last, norm_first, 0)
     for load in loads[:2]:
         load.wait()
-    last = tile_rows - 1
 
     def first_keys(i, carry):
-        @pl.when(i > 0)
-        def _():
-            load_rows(i).wait()
-
-        project_keys(xbuf, i * TH, i + 1)
+        normed = obuf[pl.ds(i * TH, TH)].reshape(slab, feat)
+        result = lax.dot_general(normed, w_s[PADDED:, :], NT, preferred_element_type=F32)
+        kbuf[i + 1] = result[:, :PADDED].astype(BF16)
+        vbuf[i + 1] = result[:, PADDED:].astype(BF16)
         return carry
 
     lax.fori_loop(0, last, first_keys, 0)
     for load in loads[2:6]:
         load.wait()
+    normed = obuf[TH : 2 * TH].reshape(slab, feat)
+    result = lax.dot_general(normed, w_s[:PADDED, :], NT, preferred_element_type=F32)
+    qbuf[1] = (result * SCALE).astype(BF16)
 
     send_down = pltpu.make_async_remote_copy(
         x_hbm.at[pl.ds(last * TH, TH)], halo.at[0], halo_send.at[0], halo_recv.at[0],
@@ -310,7 +315,7 @@
         send_down.start()
         send_up.start()
 
-    spatial(1, lambda half: project_queries(1, 2 * half, 2 * half + 2), meet)
+    spatial(1, meet)
     load_rows(last).wait()
     project_keys(xbuf, last * TH, tile_rows)
 
@@ -328,7 +333,7 @@
 
         i = jnp.where(n == 0, 2, (n - 1) * last)
         project_queries(i)
-        spatial(i, lambda half: None, lambda: None)
+        spatial(i, lambda: None)
         return carry
 
     lax.fori_loop(0, last, other_rows, 0)

time: 99 us -> 99.7 us (level)
  no operation moved by 1% of the time
where the time goes in v5:
time: 99.7 us
  Pallas kernels  98.2 us (98%)
  local copies, waits for them, and re-layouts  1.41 us (1%)
    pallas_call x1, Pallas kernels, body(): pl.pallas_call(functools.partial(kernel, frames, rows_axis), out_shape=ja...  98.2 us

profile of v5, /device:TPU:8, one launch (start us, length us, event | category | flops | bytes accessed | tf_op | source)
XLA Modules:
  0.0 99.7 jit_solution(4961692902995561593)
XLA Ops:
  0.0 98.2 %shard_map.73 = bf16[16,64,1152]{2,1,0:T(8,128)(2,1)S(1)} custom-call(s32[9,1,16]{2,1,0:T(1,128)} %bitcast.9, s32[1,16]{1,0:T(1,128)} %counts_hbm.1, bf16[16,64,1152]{2,1,0:T(8,128)(2,1)} %bitcast.8, bf16[1728,1152]{1,0:T(8,128)(2,1)} %bitcast.6, bf16[576,1152]{1,0:T(8,128)(2,1)} %sout_hbm.1, bf16[1728,1152]{1,0:T(8,128)(2,1)} %bitcast.7, ...), custom_call_target="tpu_custom_call" | custom-call | tf_op jit(solution)/shard_map/pallas_call | solution.py:389
  98.2 1.4 %copy.9 = bf16[1,16,64,1152]{3,2,1,0:T(8,128)(2,1)} copy(bf16[1,16,64,1152]{3,2,1,0:T(8,128)(2,1)S(1)} %bitcast.5) | data formatting | bytes 4718592
